TPU v7x, 128 devices: a whole 4x4x4 slice. The times are simulated.
128 devices in a mesh: rt: 32 (over x_lo, z, y), mob: 4 (over x_hi, core).
Axes of the slice: x: 4 (x_hi: 2, x_lo: 2; x = x_hi * 2 + x_lo), y: 4, z: 4, core: 2. Of those that a mesh axis runs over, the one named last changes fastest.
Arguments:
- observed: float32 [1024, 64, 1280], P('rt', 'mob'), as said below
- frame_kernel: float32 [31], replicated, may hold values from 0.05 to 1
- scan_kernel: float32 [15], replicated, may hold values from 0.05 to 1
- prec_window: int32 [256], P('rt'), may hold values from 0 to 15
- frag_window: int32 [1024], P('mob'), may hold values from 0 to 15
Outputs:
- estimate: float32 [1024, 64, 1280], P('rt', 'mob')
- correlation: float32 [256, 1024], P('rt', 'mob')
Inputs may be any that keep to these rules, and one draw needn't show every extreme that they name: `observed`: positive intensities.
All inputs are finite; a program needn't handle non-finite values.
Results may differ from a plain program's by a relative error of at most 0.0003.
Values sent between devices are 32-bit elements; how exact they have to be, the bound alone decides.
No kernel may reach another device: no remote copies, remote signals or barrier semaphores. Data moves between devices by JAX's collectives and lax.ppermute only.
A program may use at most 64 MiB of HBM per device.

v0:
```python
import jax
import jax.numpy as jnp
from jax import lax
from jax.sharding import PartitionSpec as P

PREC = 256
ITERS = 2


def extended(cells, sides, width):
    for axis, dim in sides:
        count = lax.axis_size(axis)
        ends = count - 1
        head = lax.slice_in_dim(cells, 0, width, axis=dim)
        tail = lax.slice_in_dim(cells, cells.shape[dim] - width, cells.shape[dim], axis=dim)
        cells = jnp.concatenate(
            [
                lax.ppermute(tail, axis, [(i, (i + 1) % count) for i in range(ends)]),
                cells,
                lax.ppermute(head, axis, [((i + 1) % count, i) for i in range(ends)]),
            ],
            axis=dim,
        )
    return cells


def apply_taps(padded, kernel, along, length):
    running = kernel[0] * lax.slice_in_dim(padded, 0, length, axis=along)
    for tap_index in range(1, kernel.shape[0]):
        running = running + kernel[tap_index] * lax.slice_in_dim(
            padded, tap_index, tap_index + length, axis=along
        )
    return running


def local(observed, frame_kernel, scan_kernel, prec_window, frag_window):
    frames, scan_count, channels = observed.shape
    frame_radius = (frame_kernel.shape[0] - 1) // 2
    scan_radius = (scan_kernel.shape[0] - 1) // 2
    flip_frames = frame_kernel[::-1]
    flip_scans = scan_kernel[::-1]
    estimate = observed
    for iteration in range(ITERS):
        padded_scans = extended(estimate, (("mob", 1),), scan_radius)
        scan_blurred = apply_taps(padded_scans, scan_kernel, 1, scan_count)
        padded_frames = extended(scan_blurred, (("rt", 0),), frame_radius)
        blurred_image = apply_taps(padded_frames, frame_kernel, 0, frames)
        ratio_field = observed / blurred_image
        ratio_frames = extended(ratio_field, (("rt", 0),), frame_radius)
        scan_padded_scans = extended(
            apply_taps(ratio_frames, flip_frames, 0, frames), (("mob", 1),), scan_radius
        )
        estimate = estimate * apply_taps(scan_padded_scans, flip_scans, 1, scan_count)
    profiles = estimate.reshape(frames * scan_count, channels)
    cell_count = frames * scan_count * lax.axis_size("rt") * lax.axis_size("mob")
    channel_total = lax.psum(jnp.sum(profiles, axis=0), ("rt", "mob"))
    channel_mean = channel_total / cell_count
    centered = (profiles - channel_mean).astype(jnp.bfloat16)
    as_float = centered.astype(jnp.float32)
    squares = lax.psum(jnp.sum(as_float * as_float, axis=0), ("rt", "mob"))
    cross_sums = lax.dot_general(
        centered[:, :PREC],
        centered[:, PREC:],
        (((0,), (0,)), ((), ())),
        preferred_element_type=jnp.float32,
    )
    partial_value = lax.psum_scatter(cross_sums, "rt", scatter_dimension=0, tiled=True)
    block_sums = lax.psum_scatter(partial_value, "mob", scatter_dimension=1, tiled=True)
    row_count = prec_window.shape[0]
    column_count = frag_window.shape[0]
    inverse_norm = 1.0 / jnp.sqrt(squares + 1e-06)
    row_inverse = lax.dynamic_slice_in_dim(
        inverse_norm[:PREC], lax.axis_index("rt") * row_count, row_count
    )
    column_inverse = lax.dynamic_slice_in_dim(
        inverse_norm[PREC:], lax.axis_index("mob") * column_count, column_count
    )
    pair_mask = (prec_window[:, None] == frag_window[None, :]).astype(jnp.float32)
    correlation = pair_mask * block_sums * row_inverse[:, None] * column_inverse[None, :]
    return (estimate, correlation)


def solution(mesh):
    placed = (P("rt", "mob", None), P(), P(), P("rt"), P("mob"))
    return jax.shard_map(
        local,
        mesh=mesh,
        in_specs=placed,
        out_specs=(P("rt", "mob", None), P("rt", "mob")),
        check_vma=False,
    )
```

profile of v0, /device:TPU:1, one launch (start us, length us, event | category | flops | bytes accessed | tf_op | source)
XLA Modules:
  0.0 732.5 jit_solution(15922620967570289949)
XLA Ops:
  9.5 6.2 collective-permute-start
  18.9 9.5 %collective-permute-done = f32[32,7,1280]{2,0,1:T(8,128)S(1)} collective-permute-done((f32[32,7,1280]{2,0,1:T(8,128)S(1)}, f32[32,7,1280]{2,0,1:T(8,128)S(1)}, u32[]{:S(2)}, u32[]{:S(2)}) %collective-permute-start) | collective-permute-done | bytes 1146912 | tf_op jit(solution)/shard_map/ppermute | solution.py:18
  29.1 5.6 collective-permute-done.1
  35.4 15.1 %fusion.127 = f32[32,16,1280]{2,1,0:T(8,128)S(1)} fusion(f32[32,16,1280]{2,1,0:T(8,128)S(1)} %copy-done, f32[32,7,1280]{2,1,0:T(8,128)S(1)} %copy.17, f32[32,23,1280]{2,1,0:T(8,128)S(1)} %copy_dynamic-update-slice_fusion, f32[]{:T(128)} %bitcast.16, f32[]{:T(128)} %bitcast.15, f32[]{:T(128)} %bitcast.14, f32[]{:T(128)} %bitcast.13, f32[]{:T(128)} %bitcast.12, ...), kind=kLoop, calls=%fused_computation.435 | loop fusion | flops 23592960 | bytes 24739900 | tf_op jit(solution)/shard_map/add | solution.py:30
  56.7 10.9 %collective-permute-done.2 = f32[15,16,1280]{2,1,0:T(8,128)S(1)} collective-permute-done((f32[15,16,1280]{2,1,0:T(8,128)S(1)}, f32[15,16,1280]{2,1,0:T(8,128)S(1)}, u32[]{:S(2)}, u32[]{:S(2)}) %collective-permute-start.2) | collective-permute-done | bytes 1228832 | tf_op jit(solution)/shard_map/ppermute | solution.py:18
  67.5 3.9 collective-permute-done.3
  72.5 34.5 %fusion.405 = f32[32,16,1280]{2,1,0:T(8,128)} fusion(f32[32,16,1280]{2,1,0:T(8,128)S(1)} %copy-done, f32[32,16,1280]{2,1,0:T(8,128)S(1)} %fusion.127, f32[15,16,1280]{2,1,0:T(8,128)} %copy-done.5, f32[15,16,1280]{2,1,0:T(8,128)S(1)} %collective-permute-done.2, f32[]{:T(128)} %bitcast.45, f32[]{:T(128)} %bitcast.44, f32[]{:T(128)} %bitcast.43, f32[]{:T(128)} %bitcast.42, ...), kind=kLoop, calls=%fused_computation.713 | loop fusion | flops 60293120 | bytes 10322044 | tf_op jit(solution)/shard_map/div | solution.py:48
  113.3 13.4 %collective-permute-done.4 = f32[15,16,1280]{2,1,0:T(8,128)S(1)} collective-permute-done((f32[15,16,1280]{2,1,0:T(8,128)S(1)}, f32[15,16,1280]{2,1,0:T(8,128)S(1)}, u32[]{:S(2)}, u32[]{:S(2)}) %collective-permute-start.4) | collective-permute-done | bytes 1228832 | tf_op jit(solution)/shard_map/ppermute | solution.py:18
  126.7 4.3 collective-permute-done.5
  130.9 53.8 %fusion.318 = f32[32,16,1280]{2,1,0:T(8,128)S(1)} fusion(f32[32,16,1280]{2,1,0:T(8,128)} %fusion.405, f32[15,16,1280]{2,1,0:T(8,128)} %collective-permute-done.5, f32[15,16,1280]{2,1,0:T(8,128)S(1)} %collective-permute-done.4, f32[]{:T(128)} %bitcast.45, f32[]{:T(128)} %bitcast.44, f32[]{:T(128)} %bitcast.43, f32[]{:T(128)} %bitcast.42, f32[]{:T(128)} %bitcast.41, ...), kind=kLoop, calls=%fused_computation.626 | loop fusion | flops 59637760 | bytes 7700604 | tf_op jit(solution)/shard_map/add | solution.py:30
  186.6 3.4 collective-permute-start.6
  192.6 10.0 %collective-permute-done.6 = f32[32,7,1280]{2,0,1:T(8,128)S(1)} collective-permute-done((f32[32,7,1280]{2,0,1:T(8,128)S(1)}, f32[32,7,1280]{2,0,1:T(8,128)S(1)}, u32[]{:S(2)}, u32[]{:S(2)}) %collective-permute-start.6) | collective-permute-done | bytes 1146912 | tf_op jit(solution)/shard_map/ppermute | solution.py:18
  203.3 6.1 collective-permute-done.7
  210.0 16.5 %fusion.81 = f32[32,16,1280]{2,1,0:T(8,128)S(1)} fusion(f32[32,16,1280]{2,1,0:T(8,128)S(1)} %copy-done, f32[32,16,1280]{2,1,0:T(8,128)S(1)} %copy-done.3, f32[32,7,1280]{2,1,0:T(8,128)S(1)} %copy.23, f32[32,7,1280]{2,1,0:T(8,128)S(1)} %copy.21, f32[]{:T(128)} %bitcast.16, f32[]{:T(128)} %bitcast.15, f32[]{:T(128)} %bitcast.14, f32[]{:T(128)} %bitcast.13, ...), kind=kLoop, calls=%fused_computation.389 | loop fusion | flops 28835840 | bytes 10158140 | tf_op jit(solution)/shard_map/mul | solution.py:53
  231.9 9.9 %collective-permute-done.8 = f32[32,7,1280]{2,0,1:T(8,128)S(1)} collective-permute-done((f32[32,7,1280]{2,0,1:T(8,128)S(1)}, f32[32,7,1280]{2,0,1:T(8,128)S(1)}, u32[]{:S(2)}, u32[]{:S(2)}) %collective-permute-start.8) | collective-permute-done | bytes 1146912 | tf_op jit(solution)/shard_map/ppermute | solution.py:18
  242.5 5.6 collective-permute-done.9
  248.8 16.3 %fusion.42 = f32[32,16,1280]{2,1,0:T(8,128)S(1)} fusion(f32[32,16,1280]{2,1,0:T(8,128)S(1)} %fusion.81, f32[32,7,1280]{2,1,0:T(8,128)S(1)} %copy.27, f32[32,7,1280]{2,1,0:T(8,128)S(1)} %copy.25, f32[]{:T(128)} %bitcast.16, f32[]{:T(128)} %bitcast.15, f32[]{:T(128)} %bitcast.14, f32[]{:T(128)} %bitcast.13, f32[]{:T(128)} %bitcast.12, f32[]{:T(128)} %bitcast.11, ...), kind=kLoop, calls=%fused_computation.350 | loop fusion | flops 28180480 | bytes 7536700 | tf_op jit(solution)/shard_map/add | solution.py:30
  266.8 4.6 collective-permute-start.10
  272.7 12.5 %collective-permute-done.10 = f32[15,16,1280]{2,1,0:T(8,128)S(1)} collective-permute-done((f32[15,16,1280]{2,1,0:T(8,128)S(1)}, f32[15,16,1280]{2,1,0:T(8,128)S(1)}, u32[]{:S(2)}, u32[]{:S(2)}) %collective-permute-start.10) | collective-permute-done | bytes 1228832 | tf_op jit(solution)/shard_map/ppermute | solution.py:18
  285.2 4.3 collective-permute-done.11
  289.4 54.3 %fusion.232 = f32[32,16,1280]{2,1,0:T(8,128)} fusion(f32[32,16,1280]{2,1,0:T(8,128)S(1)} %copy-done, f32[32,16,1280]{2,1,0:T(8,128)} %copy-done.4, f32[15,16,1280]{2,1,0:T(8,128)} %collective-permute-done.11, f32[15,16,1280]{2,1,0:T(8,128)S(1)} %collective-permute-done.10, f32[]{:T(128)} %bitcast.45, f32[]{:T(128)} %bitcast.44, f32[]{:T(128)} %bitcast.43, ...), kind=kLoop, calls=%fused_computation.540 | loop fusion | flops 60293120 | bytes 10322044 | tf_op jit(solution)/shard_map/div | solution.py:48
  345.6 3.8 collective-permute-start.12
  350.8 13.4 %collective-permute-done.12 = f32[15,16,1280]{2,1,0:T(8,128)S(1)} collective-permute-done((f32[15,16,1280]{2,1,0:T(8,128)S(1)}, f32[15,16,1280]{2,1,0:T(8,128)S(1)}, u32[]{:S(2)}, u32[]{:S(2)}) %collective-permute-start.12) | collective-permute-done | bytes 1228832 | tf_op jit(solution)/shard_map/ppermute | solution.py:18
  364.3 4.5 collective-permute-done.13
  368.8 52.5 %fusion.145 = f32[32,16,1280]{2,1,0:T(8,128)S(1)} fusion(f32[32,16,1280]{2,1,0:T(8,128)} %fusion.232, f32[15,16,1280]{2,1,0:T(8,128)} %collective-permute-done.13, f32[15,16,1280]{2,1,0:T(8,128)S(1)} %collective-permute-done.12, f32[]{:T(128)} %bitcast.45, f32[]{:T(128)} %bitcast.44, f32[]{:T(128)} %bitcast.43, f32[]{:T(128)} %bitcast.42, f32[]{:T(128)} %bitcast.41, ...), kind=kLoop, calls=%fused_computation.453 | loop fusion | flops 59637760 | bytes 7700604 | tf_op jit(solution)/shard_map/add | solution.py:30
  426.7 10.3 %collective-permute-done.14 = f32[32,7,1280]{2,0,1:T(8,128)S(1)} collective-permute-done((f32[32,7,1280]{2,0,1:T(8,128)S(1)}, f32[32,7,1280]{2,0,1:T(8,128)S(1)}, u32[]{:S(2)}, u32[]{:S(2)}) %collective-permute-start.14) | collective-permute-done | bytes 1146912 | tf_op jit(solution)/shard_map/ppermute | solution.py:18
  437.6 5.6 collective-permute-done.15
  443.9 17.4 %fusion.507 = (f32[1280]{0:T(1024)S(1)}, f32[32,16,1280]{2,1,0:T(8,128)}) fusion(f32[32,16,1280]{2,1,0:T(8,128)S(1)} %fusion.81, f32[32,7,1280]{2,1,0:T(8,128)S(1)} %copy.31, f32[32,16,1280]{2,1,0:T(8,128)S(1)} %fusion.145, f32[]{:T(128)} %bitcast.3, f32[]{:T(128)} %bitcast.4, f32[]{:T(128)} %bitcast.5, f32[]{:T(128)} %bitcast.6, f32[]{:T(128)} %bitcast.7, ...), kind=kLoop, calls=%fused_computation.845 | loop fusion | flops 29489920 | bytes 10163260 | tf_op jit(solution)/shard_map/reduce_sum | solution.py:56
  461.3 74.5 %psum.14 = f32[1280]{0:T(1024)S(1)} all-reduce(f32[1280]{0:T(1024)S(1)} %get-tuple-element.4), channel_id=1, replica_groups=mesh['rt'=32,'mob'=4] {'rt','mob'}, use_global_device_ids=true, to_apply=%region_1.0 | all-reduce | flops 1280 | bytes 10240 | tf_op jit(solution)/shard_map/psum | solution.py:56
  540.2 64.9 %psum.15 = f32[1280]{0:T(1024)S(1)} all-reduce(f32[1280]{0:T(1024)S(1)} %multiply_reduce_fusion), channel_id=1, replica_groups=mesh['rt'=32,'mob'=4] {'rt','mob'}, use_global_device_ids=true, to_apply=%region_5.0 | all-reduce | flops 1280 | bytes 10240 | tf_op jit(solution)/shard_map/psum | solution.py:60
  605.2 69.0 %reduce-scatter.3.cloned.1.call-done = f32[8,1024]{1,0:T(8,128)} async-done(((f32[256,1024]{1,0:T(8,128)}), f32[8,1024]{1,0:T(8,128)}) %reduce-scatter.3.cloned.1.call-update) | async-done | bytes 32784 | tf_op jit(solution)/shard_map/reduce_scatter | solution.py:67
  674.4 49.9 %reduce-scatter.5.cloned.1.call-done = f32[8,256]{1,0:T(8,128)} async-done(((f32[8,1024]{1,0:T(8,128)}), f32[8,256]{1,0:T(8,128)}) %reduce-scatter.5.cloned.1.call-update) | async-done | bytes 8208 | tf_op jit(solution)/shard_map/reduce_scatter | solution.py:68
  (74 shorter events, 51.7 us)
Async XLA Ops:
  7.2 667.0 %reduce-scatter.3.cloned.1.call-start = ((), (), s32[]{:S(2)}) async-start(), calls=%async_computation.2 | async-start | bytes 1081344 | tf_op jit(solution)/shard_map/reduce_scatter | solution.py:67
  9.1 8.9 %copy-start.7 = (f32[15]{0:T(128)S(1)}, f32[15]{0:T(128)}, u32[]{:S(2)}) copy-start(f32[15]{0:T(128)} %param.7) | copy-start | bytes 184
  9.1 9.6 %copy-start = (f32[32,16,1280]{2,1,0:T(8,128)S(1)}, f32[32,16,1280]{2,1,0:T(8,128)}, u32[]{:S(2)}) copy-start(f32[32,16,1280]{2,1,0:T(8,128)} %param.5) | copy-start | bytes 7864324
  9.5 18.9 %collective-permute-start = (f32[32,7,1280]{2,0,1:T(8,128)S(1)}, f32[32,7,1280]{2,0,1:T(8,128)S(1)}, u32[]{:S(2)}, u32[]{:S(2)}) collective-permute-start(f32[32,7,1280]{2,0,1:T(8,128)S(1)} %copy.32), channel_id=1, source_target_pairs={{0,1},{1,2},{2,3},{4,5},{5,6},{6,7},{8,9},{9,10},{10,11},{12,13},{... | collective-permute-start | bytes 3440648 | tf_op jit(solution)/shard_map/ppermute | solution.py:18
  16.0 18.7 %collective-permute-start.1 = (f32[32,7,1280]{2,0,1:T(8,128)S(1)}, f32[32,7,1280]{2,0,1:T(8,128)S(1)}, u32[]{:S(2)}, u32[]{:S(2)}) collective-permute-start(f32[32,7,1280]{2,0,1:T(8,128)S(1)} %copy.33), channel_id=1, source_target_pairs={{1,0},{2,1},{3,2},{5,4},{6,5},{7,6},{9,8},{10,9},{11,10},{13,12},{... | collective-permute-start | bytes 3440648 | tf_op jit(solution)/shard_map/ppermute | solution.py:20
  50.5 4.8 copy-start.6
  50.7 16.9 %collective-permute-start.2 = (f32[15,16,1280]{2,1,0:T(8,128)S(1)}, f32[15,16,1280]{2,1,0:T(8,128)S(1)}, u32[]{:S(2)}, u32[]{:S(2)}) collective-permute-start(f32[15,16,1280]{2,1,0:T(8,128)S(1)} %get-tuple-element.18), channel_id=1, source_target_pairs={{0,4},{4,8},{8,12},{12,16},{16,20},{20,24},{24,28},{28,32},{32,36}... | collective-permute-start | bytes 3686408 | tf_op jit(solution)/shard_map/ppermute | solution.py:18
  53.9 17.5 %collective-permute-start.3 = (f32[15,16,1280]{2,1,0:T(8,128)S(1)}, f32[15,16,1280]{2,1,0:T(8,128)S(1)}, u32[]{:S(2)}, u32[]{:S(2)}) collective-permute-start(f32[15,16,1280]{2,1,0:T(8,128)S(1)} %get-tuple-element.19), channel_id=1, source_target_pairs={{4,0},{8,4},{12,8},{16,12},{20,16},{24,20},{28,24},{32,28},{36,32}... | collective-permute-start | bytes 3686408 | tf_op jit(solution)/shard_map/ppermute | solution.py:20
  71.4 1.1 copy-start.5
  108.8 17.9 %collective-permute-start.4 = (f32[15,16,1280]{2,1,0:T(8,128)S(1)}, f32[15,16,1280]{2,1,0:T(8,128)S(1)}, u32[]{:S(2)}, u32[]{:S(2)}) collective-permute-start(f32[15,16,1280]{2,1,0:T(8,128)S(1)} %get-tuple-element.16), channel_id=1, source_target_pairs={{0,4},{4,8},{8,12},{12,16},{16,20},{20,24},{24,28},{28,32},{32,36}... | collective-permute-start | bytes 3686408 | tf_op jit(solution)/shard_map/ppermute | solution.py:18
  112.0 18.9 %collective-permute-start.5 = (f32[15,16,1280]{2,1,0:T(8,128)S(1)}, f32[15,16,1280]{2,1,0:T(8,128)}, u32[]{:S(2)}, u32[]{:S(2)}) collective-permute-start(f32[15,16,1280]{2,1,0:T(8,128)S(1)} %get-tuple-element.17), channel_id=1, source_target_pairs={{4,0},{8,4},{12,8},{16,12},{20,16},{24,20},{28,24},{32,28},{36,32}... | collective-permute-start | bytes 3686408 | tf_op jit(solution)/shard_map/ppermute | solution.py:20
  184.7 1.5 copy-start.2
  186.6 16.0 %collective-permute-start.6 = (f32[32,7,1280]{2,0,1:T(8,128)S(1)}, f32[32,7,1280]{2,0,1:T(8,128)S(1)}, u32[]{:S(2)}, u32[]{:S(2)}) collective-permute-start(f32[32,7,1280]{2,0,1:T(8,128)S(1)} %copy.20), channel_id=1, source_target_pairs={{0,1},{1,2},{2,3},{4,5},{5,6},{6,7},{8,9},{9,10},{10,11},{12,13},{... | collective-permute-start | bytes 3440648 | tf_op jit(solution)/shard_map/ppermute | solution.py:18
  190.4 19.6 %copy-start.3 = (f32[32,16,1280]{2,1,0:T(8,128)S(1)}, f32[32,16,1280]{2,1,0:T(8,128)}, u32[]{:S(2)}) copy-start(f32[32,16,1280]{2,1,0:T(8,128)} %copy-done.2) | copy-start | bytes 7864324
  190.4 18.9 %collective-permute-start.7 = (f32[32,7,1280]{2,0,1:T(8,128)S(1)}, f32[32,7,1280]{2,0,1:T(8,128)S(1)}, u32[]{:S(2)}, u32[]{:S(2)}) collective-permute-start(f32[32,7,1280]{2,0,1:T(8,128)S(1)} %copy.22), channel_id=1, source_target_pairs={{1,0},{2,1},{3,2},{5,4},{6,5},{7,6},{9,8},{10,9},{11,10},{13,12},{... | collective-permute-start | bytes 3440648 | tf_op jit(solution)/shard_map/ppermute | solution.py:20
  227.2 14.7 %collective-permute-start.8 = (f32[32,7,1280]{2,0,1:T(8,128)S(1)}, f32[32,7,1280]{2,0,1:T(8,128)S(1)}, u32[]{:S(2)}, u32[]{:S(2)}) collective-permute-start(f32[32,7,1280]{2,0,1:T(8,128)S(1)} %copy.24), channel_id=1, source_target_pairs={{0,1},{1,2},{2,3},{4,5},{5,6},{6,7},{8,9},{9,10},{10,11},{12,13},{... | collective-permute-start | bytes 3440648 | tf_op jit(solution)/shard_map/ppermute | solution.py:18
  229.5 18.7 %collective-permute-start.9 = (f32[32,7,1280]{2,0,1:T(8,128)S(1)}, f32[32,7,1280]{2,0,1:T(8,128)S(1)}, u32[]{:S(2)}, u32[]{:S(2)}) collective-permute-start(f32[32,7,1280]{2,0,1:T(8,128)S(1)} %copy.26), channel_id=1, source_target_pairs={{1,0},{2,1},{3,2},{5,4},{6,5},{7,6},{9,8},{10,9},{11,10},{13,12},{... | collective-permute-start | bytes 3440648 | tf_op jit(solution)/shard_map/ppermute | solution.py:20
  265.1 1.5 copy-start.4
  266.8 18.4 %collective-permute-start.10 = (f32[15,16,1280]{2,1,0:T(8,128)S(1)}, f32[15,16,1280]{2,1,0:T(8,128)S(1)}, u32[]{:S(2)}, u32[]{:S(2)}) collective-permute-start(f32[15,16,1280]{2,1,0:T(8,128)S(1)} %get-tuple-element.10), channel_id=1, source_target_pairs={{0,4},{4,8},{8,12},{12,16},{16,20},{20,24},{24,28},{28,32},{32,36}... | collective-permute-start | bytes 3686408 | tf_op jit(solution)/shard_map/ppermute | solution.py:18
  271.4 18.1 %collective-permute-start.11 = (f32[15,16,1280]{2,1,0:T(8,128)S(1)}, f32[15,16,1280]{2,1,0:T(8,128)}, u32[]{:S(2)}, u32[]{:S(2)}) collective-permute-start(f32[15,16,1280]{2,1,0:T(8,128)S(1)} %get-tuple-element.11), channel_id=1, source_target_pairs={{4,0},{8,4},{12,8},{16,12},{20,16},{24,20},{28,24},{32,28},{36,32}... | collective-permute-start | bytes 3686408 | tf_op jit(solution)/shard_map/ppermute | solution.py:20
  345.6 18.7 %collective-permute-start.12 = (f32[15,16,1280]{2,1,0:T(8,128)S(1)}, f32[15,16,1280]{2,1,0:T(8,128)S(1)}, u32[]{:S(2)}, u32[]{:S(2)}) collective-permute-start(f32[15,16,1280]{2,1,0:T(8,128)S(1)} %get-tuple-element.8), channel_id=1, source_target_pairs={{0,4},{4,8},{8,12},{12,16},{16,20},{20,24},{24,28},{28,32},{32,36}... | collective-permute-start | bytes 3686408 | tf_op jit(solution)/shard_map/ppermute | solution.py:18
  349.3 19.4 %collective-permute-start.13 = (f32[15,16,1280]{2,1,0:T(8,128)S(1)}, f32[15,16,1280]{2,1,0:T(8,128)}, u32[]{:S(2)}, u32[]{:S(2)}) collective-permute-start(f32[15,16,1280]{2,1,0:T(8,128)S(1)} %get-tuple-element.9), channel_id=1, source_target_pairs={{4,0},{8,4},{12,8},{16,12},{20,16},{24,20},{28,24},{32,28},{36,32}... | collective-permute-start | bytes 3686408 | tf_op jit(solution)/shard_map/ppermute | solution.py:20
  421.9 15.1 %collective-permute-start.14 = (f32[32,7,1280]{2,0,1:T(8,128)S(1)}, f32[32,7,1280]{2,0,1:T(8,128)S(1)}, u32[]{:S(2)}, u32[]{:S(2)}) collective-permute-start(f32[32,7,1280]{2,0,1:T(8,128)S(1)} %copy.28), channel_id=1, source_target_pairs={{0,1},{1,2},{2,3},{4,5},{5,6},{6,7},{8,9},{9,10},{10,11},{12,13},{... | collective-permute-start | bytes 3440648 | tf_op jit(solution)/shard_map/ppermute | solution.py:18
  424.6 18.7 %collective-permute-start.15 = (f32[32,7,1280]{2,0,1:T(8,128)S(1)}, f32[32,7,1280]{2,0,1:T(8,128)S(1)}, u32[]{:S(2)}, u32[]{:S(2)}) collective-permute-start(f32[32,7,1280]{2,0,1:T(8,128)S(1)} %copy.30), channel_id=1, source_target_pairs={{1,0},{2,1},{3,2},{5,4},{6,5},{7,6},{9,8},{10,9},{11,10},{13,12},{... | collective-permute-start | bytes 3440648 | tf_op jit(solution)/shard_map/ppermute | solution.py:20
  537.8 2.1 copy-start.1
  537.8 186.5 %copy-start.8 = (s32[256]{0:T(256)S(1)}, s32[256]{0:T(256)}, u32[]{:S(2)}) copy-start(s32[256]{0:T(256)} %param.9) | copy-start | bytes 3076
  537.8 186.5 %copy-start.9 = (s32[8]{0:T(128)S(1)}, s32[8]{0:T(128)}, u32[]{:S(2)}) copy-start(s32[8]{0:T(128)} %param.8) | copy-start | bytes 100
  539.3 185.0 %reduce-scatter.5.cloned.1.call-start = ((), (), s32[]{:S(2)}) async-start(), calls=%async_computation.3 | async-start | bytes 40960 | tf_op jit(solution)/shard_map/reduce_scatter | solution.py:68
Sparse Core Ops, SparseCore 0:
  539.4 134.6 reduce-scatter.2
  676.6 47.5 reduce-scatter.4
where the time goes:
time: 735 us; the launch traced here: 733 us
  other arithmetic  264 us (36%)
  waiting for transfers between devices  249 us (34%)
  blocking collectives  139 us (19%)
  starting transfers between devices  42.8 us (6%)
  local copies, waits for them, and re-layouts  21.7 us (3%)
  between operations  14.5 us (2%)
    add x4, other arithmetic, apply_taps(): running + kernel[tap_index] * lax.slice_in_dim(padded, tap_index, tap_ind...  138 us
    ppermute x8, waiting for transfers between devices, extended(): lax.ppermute(tail, axis, [(i, (i + 1) % count) for i in range(ends)])  89.9 us
    div x2, other arithmetic, local(): ratio_field = observed / blurred_image  88.8 us
    psum x1, blocking collectives, local(): channel_total = lax.psum(jnp.sum(profiles, axis=0), ('rt', 'mob'))  74.5 us
    reduce_scatter x1, waiting for transfers between devices, local(): lax.psum_scatter(cross_sums, 'rt', scatter_dimension=0, tiled=True)  69 us
    psum x1, blocking collectives, local(): squares = lax.psum(jnp.sum(as_float * as_float, axis=0), ('rt', 'mob'))  64.9 us
    reduce_scatter x1, waiting for transfers between devices, local(): lax.psum_scatter(partial_value, 'mob', scatter_dimension=1, tiled=True)  49.9 us
    ppermute x8, waiting for transfers between devices, extended(): lax.ppermute(head, axis, [((i + 1) % count, i) for i in range(ends)])  39.8 us
  transfers between devices with their start and end apart: 18, of which 18 were waited for; matrix products, arithmetic and copies ran while one was open for 1% of the time, Pallas kernels for 0%

commit v1 on v0

--- a/solution.py
+++ b/solution.py
@@ -53,7 +53,8 @@
         estimate = estimate * apply_taps(scan_padded_scans, flip_scans, 1, scan_count)
     profiles = estimate.reshape(frames * scan_count, channels)
     cell_count = frames * scan_count * lax.axis_size("rt") * lax.axis_size("mob")
-    channel_total = lax.psum(jnp.sum(profiles, axis=0), ("rt", "mob"))
+    tell_stages_all = lambda buf: lax.psum(lax.psum(buf, "mob"), "rt")
+    channel_total = tell_stages_all(jnp.sum(profiles, axis=0))
     channel_mean = channel_total / cell_count
     centered = (profiles - channel_mean).astype(jnp.bfloat16)
     as_float = centered.astype(jnp.float32)

time: 735 us -> 759 us (1.033)
  blocking collectives: 139 us -> 164 us
    psum x1, blocking collectives: 64.9 us -> 91.1 us  [local(): squares = lax.psum(jnp.sum(as_float * as_float, axis=0), ('rt', 'mob'))]
    psum x1 -> x2, blocking collectives: 74.5 us -> 72.6 us  [local(): tell_stages_all = lambda buf: lax.psum(lax.psum(buf, 'mob'), 'rt')]
where the time goes in v1:
time: 759 us; the launch traced here: 757 us
  other arithmetic  264 us (35%)
  waiting for transfers between devices  249 us (33%)
  blocking collectives  164 us (22%)
  starting transfers between devices  42.8 us (6%)
  local copies, waits for them, and re-layouts  21.9 us (3%)
  between operations  14.5 us (2%)
    add x4, other arithmetic, apply_taps(): running + kernel[tap_index] * lax.slice_in_dim(padded, tap_index, tap_ind...  137 us
    psum x1, blocking collectives, local(): squares = lax.psum(jnp.sum(as_float * as_float, axis=0), ('rt', 'mob'))  91.1 us
    ppermute x8, waiting for transfers between devices, extended(): lax.ppermute(tail, axis, [(i, (i + 1) % count) for i in range(ends)])  89.9 us
    div x2, other arithmetic, local(): ratio_field = observed / blurred_image  89.1 us
    psum x2, blocking collectives, local(): tell_stages_all = lambda buf: lax.psum(lax.psum(buf, 'mob'), 'rt')  72.6 us
    reduce_scatter x1, waiting for transfers between devices, local(): lax.psum_scatter(cross_sums, 'rt', scatter_dimension=0, tiled=True)  70 us
    reduce_scatter x1, waiting for transfers between devices, local(): lax.psum_scatter(partial_value, 'mob', scatter_dimension=1, tiled=True)  49.3 us
    ppermute x8, waiting for transfers between devices, extended(): lax.ppermute(head, axis, [((i + 1) % count, i) for i in range(ends)])  39.8 us
  transfers between devices with their start and end apart: 18, of which 18 were waited for; matrix products, arithmetic and copies ran while one was open for 1% of the time, Pallas kernels for 0%

profile of v1, /device:TPU:1, one launch (start us, length us, event | category | flops | bytes accessed | tf_op | source)
XLA Modules:
  0.0 756.8 jit_solution(2931115726858465187)
XLA Ops:
  9.5 6.2 collective-permute-start
  18.9 9.6 %collective-permute-done = f32[32,7,1280]{2,0,1:T(8,128)S(1)} collective-permute-done((f32[32,7,1280]{2,0,1:T(8,128)S(1)}, f32[32,7,1280]{2,0,1:T(8,128)S(1)}, u32[]{:S(2)}, u32[]{:S(2)}) %collective-permute-start) | collective-permute-done | bytes 1146912 | tf_op jit(solution)/shard_map/ppermute | solution.py:18
  29.1 5.6 collective-permute-done.1
  35.4 15.0 %fusion.127 = f32[32,16,1280]{2,1,0:T(8,128)S(1)} fusion(f32[32,16,1280]{2,1,0:T(8,128)S(1)} %copy-done, f32[32,7,1280]{2,1,0:T(8,128)S(1)} %copy.17, f32[32,23,1280]{2,1,0:T(8,128)S(1)} %copy_dynamic-update-slice_fusion, f32[]{:T(128)} %bitcast.16, f32[]{:T(128)} %bitcast.15, f32[]{:T(128)} %bitcast.14, f32[]{:T(128)} %bitcast.13, f32[]{:T(128)} %bitcast.12, ...), kind=kLoop, calls=%fused_computation.435 | loop fusion | flops 23592960 | bytes 24739900 | tf_op jit(solution)/shard_map/add | solution.py:30
  56.6 10.9 %collective-permute-done.2 = f32[15,16,1280]{2,1,0:T(8,128)S(1)} collective-permute-done((f32[15,16,1280]{2,1,0:T(8,128)S(1)}, f32[15,16,1280]{2,1,0:T(8,128)S(1)}, u32[]{:S(2)}, u32[]{:S(2)}) %collective-permute-start.2) | collective-permute-done | bytes 1228832 | tf_op jit(solution)/shard_map/ppermute | solution.py:18
  67.5 3.9 collective-permute-done.3
  72.4 34.4 %fusion.405 = f32[32,16,1280]{2,1,0:T(8,128)} fusion(f32[32,16,1280]{2,1,0:T(8,128)S(1)} %copy-done, f32[32,16,1280]{2,1,0:T(8,128)S(1)} %fusion.127, f32[15,16,1280]{2,1,0:T(8,128)} %copy-done.4, f32[15,16,1280]{2,1,0:T(8,128)S(1)} %collective-permute-done.2, f32[]{:T(128)} %bitcast.45, f32[]{:T(128)} %bitcast.44, f32[]{:T(128)} %bitcast.43, f32[]{:T(128)} %bitcast.42, ...), kind=kLoop, calls=%fused_computation.713 | loop fusion | flops 60293120 | bytes 10322044 | tf_op jit(solution)/shard_map/div | solution.py:48
  113.2 13.4 %collective-permute-done.4 = f32[15,16,1280]{2,1,0:T(8,128)S(1)} collective-permute-done((f32[15,16,1280]{2,1,0:T(8,128)S(1)}, f32[15,16,1280]{2,1,0:T(8,128)S(1)}, u32[]{:S(2)}, u32[]{:S(2)}) %collective-permute-start.4) | collective-permute-done | bytes 1228832 | tf_op jit(solution)/shard_map/ppermute | solution.py:18
  126.6 4.3 collective-permute-done.5
  130.9 52.8 %fusion.318 = f32[32,16,1280]{2,1,0:T(8,128)S(1)} fusion(f32[32,16,1280]{2,1,0:T(8,128)} %fusion.405, f32[15,16,1280]{2,1,0:T(8,128)} %collective-permute-done.5, f32[15,16,1280]{2,1,0:T(8,128)S(1)} %collective-permute-done.4, f32[]{:T(128)} %bitcast.45, f32[]{:T(128)} %bitcast.44, f32[]{:T(128)} %bitcast.43, f32[]{:T(128)} %bitcast.42, f32[]{:T(128)} %bitcast.41, ...), kind=kLoop, calls=%fused_computation.626 | loop fusion | flops 59637760 | bytes 7700604 | tf_op jit(solution)/shard_map/add | solution.py:30
  191.5 10.0 %collective-permute-done.6 = f32[32,7,1280]{2,0,1:T(8,128)S(1)} collective-permute-done((f32[32,7,1280]{2,0,1:T(8,128)S(1)}, f32[32,7,1280]{2,0,1:T(8,128)S(1)}, u32[]{:S(2)}, u32[]{:S(2)}) %collective-permute-start.6) | collective-permute-done | bytes 1146912 | tf_op jit(solution)/shard_map/ppermute | solution.py:18
  202.2 6.1 collective-permute-done.7
  209.0 16.4 %fusion.81 = f32[32,16,1280]{2,1,0:T(8,128)S(1)} fusion(f32[32,16,1280]{2,1,0:T(8,128)S(1)} %copy-done, f32[32,16,1280]{2,1,0:T(8,128)S(1)} %copy-done.3, f32[32,7,1280]{2,1,0:T(8,128)S(1)} %copy.23, f32[32,7,1280]{2,1,0:T(8,128)S(1)} %copy.21, f32[]{:T(128)} %bitcast.16, f32[]{:T(128)} %bitcast.15, f32[]{:T(128)} %bitcast.14, f32[]{:T(128)} %bitcast.13, ...), kind=kLoop, calls=%fused_computation.389 | loop fusion | flops 28835840 | bytes 10158140 | tf_op jit(solution)/shard_map/mul | solution.py:53
  230.8 9.9 %collective-permute-done.8 = f32[32,7,1280]{2,0,1:T(8,128)S(1)} collective-permute-done((f32[32,7,1280]{2,0,1:T(8,128)S(1)}, f32[32,7,1280]{2,0,1:T(8,128)S(1)}, u32[]{:S(2)}, u32[]{:S(2)}) %collective-permute-start.8) | collective-permute-done | bytes 1146912 | tf_op jit(solution)/shard_map/ppermute | solution.py:18
  241.4 5.6 collective-permute-done.9
  247.7 17.1 %fusion.42 = f32[32,16,1280]{2,1,0:T(8,128)} fusion(f32[32,16,1280]{2,1,0:T(8,128)S(1)} %fusion.81, f32[32,7,1280]{2,1,0:T(8,128)S(1)} %copy.27, f32[32,7,1280]{2,1,0:T(8,128)S(1)} %copy.25, f32[]{:T(128)} %bitcast.16, f32[]{:T(128)} %bitcast.15, f32[]{:T(128)} %bitcast.14, f32[]{:T(128)} %bitcast.13, f32[]{:T(128)} %bitcast.12, f32[]{:T(128)} %bitcast.11, ...), kind=kLoop, calls=%fused_computation.350 | loop fusion | flops 28180480 | bytes 7536700 | tf_op jit(solution)/shard_map/add | solution.py:30
  266.5 4.6 collective-permute-start.10
  272.4 12.5 %collective-permute-done.10 = f32[15,16,1280]{2,1,0:T(8,128)S(1)} collective-permute-done((f32[15,16,1280]{2,1,0:T(8,128)S(1)}, f32[15,16,1280]{2,1,0:T(8,128)S(1)}, u32[]{:S(2)}, u32[]{:S(2)}) %collective-permute-start.10) | collective-permute-done | bytes 1228832 | tf_op jit(solution)/shard_map/ppermute | solution.py:18
  284.9 4.3 collective-permute-done.11
  289.2 54.7 %fusion.232 = f32[32,16,1280]{2,1,0:T(8,128)} fusion(f32[32,16,1280]{2,1,0:T(8,128)S(1)} %copy-done, f32[32,16,1280]{2,1,0:T(8,128)} %fusion.42, f32[15,16,1280]{2,1,0:T(8,128)} %collective-permute-done.11, f32[15,16,1280]{2,1,0:T(8,128)S(1)} %collective-permute-done.10, f32[]{:T(128)} %bitcast.45, f32[]{:T(128)} %bitcast.44, f32[]{:T(128)} %bitcast.43, ...), kind=kLoop, calls=%fused_computation.540 | loop fusion | flops 60293120 | bytes 10322044 | tf_op jit(solution)/shard_map/div | solution.py:48
  345.8 3.8 collective-permute-start.12
  351.0 13.4 %collective-permute-done.12 = f32[15,16,1280]{2,1,0:T(8,128)S(1)} collective-permute-done((f32[15,16,1280]{2,1,0:T(8,128)S(1)}, f32[15,16,1280]{2,1,0:T(8,128)S(1)}, u32[]{:S(2)}, u32[]{:S(2)}) %collective-permute-start.12) | collective-permute-done | bytes 1228832 | tf_op jit(solution)/shard_map/ppermute | solution.py:18
  364.5 4.5 collective-permute-done.13
  368.9 52.2 %fusion.145 = f32[32,16,1280]{2,1,0:T(8,128)S(1)} fusion(f32[32,16,1280]{2,1,0:T(8,128)} %fusion.232, f32[15,16,1280]{2,1,0:T(8,128)} %collective-permute-done.13, f32[15,16,1280]{2,1,0:T(8,128)S(1)} %collective-permute-done.12, f32[]{:T(128)} %bitcast.45, f32[]{:T(128)} %bitcast.44, f32[]{:T(128)} %bitcast.43, f32[]{:T(128)} %bitcast.42, f32[]{:T(128)} %bitcast.41, ...), kind=kLoop, calls=%fused_computation.453 | loop fusion | flops 59637760 | bytes 7700604 | tf_op jit(solution)/shard_map/add | solution.py:30
  426.5 10.3 %collective-permute-done.14 = f32[32,7,1280]{2,0,1:T(8,128)S(1)} collective-permute-done((f32[32,7,1280]{2,0,1:T(8,128)S(1)}, f32[32,7,1280]{2,0,1:T(8,128)S(1)}, u32[]{:S(2)}, u32[]{:S(2)}) %collective-permute-start.14) | collective-permute-done | bytes 1146912 | tf_op jit(solution)/shard_map/ppermute | solution.py:18
  437.5 5.6 collective-permute-done.15
  443.7 17.3 %fusion.507 = (f32[1280]{0:T(1024)S(1)}, f32[32,16,1280]{2,1,0:T(8,128)}) fusion(f32[32,16,1280]{2,1,0:T(8,128)S(1)} %fusion.81, f32[32,7,1280]{2,1,0:T(8,128)S(1)} %copy.31, f32[32,16,1280]{2,1,0:T(8,128)S(1)} %fusion.145, f32[]{:T(128)} %bitcast.3, f32[]{:T(128)} %bitcast.4, f32[]{:T(128)} %bitcast.5, f32[]{:T(128)} %bitcast.6, f32[]{:T(128)} %bitcast.7, ...), kind=kLoop, calls=%fused_computation.845 | loop fusion | flops 29489920 | bytes 10163260 | tf_op jit(solution)/shard_map/reduce_sum | solution.py:57
  461.0 6.7 psum.21
  467.7 65.9 %psum.22 = f32[1280]{0:T(1024)S(1)} all-reduce(f32[1280]{0:T(1024)S(1)} %psum.21), channel_id=1, replica_groups=mesh['rt'=32,'mob'=4] {'rt'}, use_global_device_ids=true, to_apply=%region_2.0 | all-reduce | flops 1280 | bytes 10240 | tf_op jit(solution)/shard_map/psum | solution.py:56
  538.0 91.1 %psum.23 = f32[1280]{0:T(1024)S(1)} all-reduce(f32[1280]{0:T(1024)S(1)} %multiply_reduce_fusion), channel_id=1, replica_groups=mesh['rt'=32,'mob'=4] {'rt','mob'}, use_global_device_ids=true, to_apply=%region_6.0 | all-reduce | flops 1280 | bytes 10240 | tf_op jit(solution)/shard_map/psum | solution.py:61
  629.1 70.0 %reduce-scatter.3.cloned.1.call-done = f32[8,1024]{1,0:T(8,128)} async-done(((f32[256,1024]{1,0:T(8,128)}), f32[8,1024]{1,0:T(8,128)}) %reduce-scatter.3.cloned.1.call-update) | async-done | bytes 32784 | tf_op jit(solution)/shard_map/reduce_scatter | solution.py:68
  699.3 49.3 %reduce-scatter.5.cloned.1.call-done = f32[8,256]{1,0:T(8,128)} async-done(((f32[8,1024]{1,0:T(8,128)}), f32[8,256]{1,0:T(8,128)}) %reduce-scatter.5.cloned.1.call-update) | async-done | bytes 8208 | tf_op jit(solution)/shard_map/reduce_scatter | solution.py:69
  (73 shorter events, 55.3 us)
Async XLA Ops:
  7.2 691.9 %reduce-scatter.3.cloned.1.call-start = ((), (), s32[]{:S(2)}) async-start(), calls=%async_computation.2 | async-start | bytes 1081344 | tf_op jit(solution)/shard_map/reduce_scatter | solution.py:68
  9.1 8.9 %copy-start.6 = (f32[15]{0:T(128)S(1)}, f32[15]{0:T(128)}, u32[]{:S(2)}) copy-start(f32[15]{0:T(128)} %param.7) | copy-start | bytes 184
  9.1 9.6 %copy-start = (f32[32,16,1280]{2,1,0:T(8,128)S(1)}, f32[32,16,1280]{2,1,0:T(8,128)}, u32[]{:S(2)}) copy-start(f32[32,16,1280]{2,1,0:T(8,128)} %param.5) | copy-start | bytes 7864324
  9.5 18.9 %collective-permute-start = (f32[32,7,1280]{2,0,1:T(8,128)S(1)}, f32[32,7,1280]{2,0,1:T(8,128)S(1)}, u32[]{:S(2)}, u32[]{:S(2)}) collective-permute-start(f32[32,7,1280]{2,0,1:T(8,128)S(1)} %copy.32), channel_id=1, source_target_pairs={{0,1},{1,2},{2,3},{4,5},{5,6},{6,7},{8,9},{9,10},{10,11},{12,13},{... | collective-permute-start | bytes 3440648 | tf_op jit(solution)/shard_map/ppermute | solution.py:18
  16.0 18.7 %collective-permute-start.1 = (f32[32,7,1280]{2,0,1:T(8,128)S(1)}, f32[32,7,1280]{2,0,1:T(8,128)S(1)}, u32[]{:S(2)}, u32[]{:S(2)}) collective-permute-start(f32[32,7,1280]{2,0,1:T(8,128)S(1)} %copy.33), channel_id=1, source_target_pairs={{1,0},{2,1},{3,2},{5,4},{6,5},{7,6},{9,8},{10,9},{11,10},{13,12},{... | collective-permute-start | bytes 3440648 | tf_op jit(solution)/shard_map/ppermute | solution.py:20
  50.5 4.8 copy-start.5
  50.6 16.9 %collective-permute-start.2 = (f32[15,16,1280]{2,1,0:T(8,128)S(1)}, f32[15,16,1280]{2,1,0:T(8,128)S(1)}, u32[]{:S(2)}, u32[]{:S(2)}) collective-permute-start(f32[15,16,1280]{2,1,0:T(8,128)S(1)} %get-tuple-element.18), channel_id=1, source_target_pairs={{0,4},{4,8},{8,12},{12,16},{16,20},{20,24},{24,28},{28,32},{32,36}... | collective-permute-start | bytes 3686408 | tf_op jit(solution)/shard_map/ppermute | solution.py:18
  53.9 17.5 %collective-permute-start.3 = (f32[15,16,1280]{2,1,0:T(8,128)S(1)}, f32[15,16,1280]{2,1,0:T(8,128)S(1)}, u32[]{:S(2)}, u32[]{:S(2)}) collective-permute-start(f32[15,16,1280]{2,1,0:T(8,128)S(1)} %get-tuple-element.19), channel_id=1, source_target_pairs={{4,0},{8,4},{12,8},{16,12},{20,16},{24,20},{28,24},{32,28},{36,32}... | collective-permute-start | bytes 3686408 | tf_op jit(solution)/shard_map/ppermute | solution.py:20
  71.4 1.1 copy-start.4
  108.7 17.9 %collective-permute-start.4 = (f32[15,16,1280]{2,1,0:T(8,128)S(1)}, f32[15,16,1280]{2,1,0:T(8,128)S(1)}, u32[]{:S(2)}, u32[]{:S(2)}) collective-permute-start(f32[15,16,1280]{2,1,0:T(8,128)S(1)} %get-tuple-element.16), channel_id=1, source_target_pairs={{0,4},{4,8},{8,12},{12,16},{16,20},{20,24},{24,28},{28,32},{32,36}... | collective-permute-start | bytes 3686408 | tf_op jit(solution)/shard_map/ppermute | solution.py:18
  111.9 18.9 %collective-permute-start.5 = (f32[15,16,1280]{2,1,0:T(8,128)S(1)}, f32[15,16,1280]{2,1,0:T(8,128)}, u32[]{:S(2)}, u32[]{:S(2)}) collective-permute-start(f32[15,16,1280]{2,1,0:T(8,128)S(1)} %get-tuple-element.17), channel_id=1, source_target_pairs={{4,0},{8,4},{12,8},{16,12},{20,16},{24,20},{28,24},{32,28},{36,32}... | collective-permute-start | bytes 3686408 | tf_op jit(solution)/shard_map/ppermute | solution.py:20
  183.7 1.5 copy-start.2
  185.5 16.0 %collective-permute-start.6 = (f32[32,7,1280]{2,0,1:T(8,128)S(1)}, f32[32,7,1280]{2,0,1:T(8,128)S(1)}, u32[]{:S(2)}, u32[]{:S(2)}) collective-permute-start(f32[32,7,1280]{2,0,1:T(8,128)S(1)} %copy.20), channel_id=1, source_target_pairs={{0,1},{1,2},{2,3},{4,5},{5,6},{6,7},{8,9},{9,10},{10,11},{12,13},{... | collective-permute-start | bytes 3440648 | tf_op jit(solution)/shard_map/ppermute | solution.py:18
  189.3 19.6 %copy-start.3 = (f32[32,16,1280]{2,1,0:T(8,128)S(1)}, f32[32,16,1280]{2,1,0:T(8,128)}, u32[]{:S(2)}) copy-start(f32[32,16,1280]{2,1,0:T(8,128)} %copy-done.2) | copy-start | bytes 7864324
  189.3 18.9 %collective-permute-start.7 = (f32[32,7,1280]{2,0,1:T(8,128)S(1)}, f32[32,7,1280]{2,0,1:T(8,128)S(1)}, u32[]{:S(2)}, u32[]{:S(2)}) collective-permute-start(f32[32,7,1280]{2,0,1:T(8,128)S(1)} %copy.22), channel_id=1, source_target_pairs={{1,0},{2,1},{3,2},{5,4},{6,5},{7,6},{9,8},{10,9},{11,10},{13,12},{... | collective-permute-start | bytes 3440648 | tf_op jit(solution)/shard_map/ppermute | solution.py:20
  226.0 14.7 %collective-permute-start.8 = (f32[32,7,1280]{2,0,1:T(8,128)S(1)}, f32[32,7,1280]{2,0,1:T(8,128)S(1)}, u32[]{:S(2)}, u32[]{:S(2)}) collective-permute-start(f32[32,7,1280]{2,0,1:T(8,128)S(1)} %copy.24), channel_id=1, source_target_pairs={{0,1},{1,2},{2,3},{4,5},{5,6},{6,7},{8,9},{9,10},{10,11},{12,13},{... | collective-permute-start | bytes 3440648 | tf_op jit(solution)/shard_map/ppermute | solution.py:18
  228.3 18.7 %collective-permute-start.9 = (f32[32,7,1280]{2,0,1:T(8,128)S(1)}, f32[32,7,1280]{2,0,1:T(8,128)S(1)}, u32[]{:S(2)}, u32[]{:S(2)}) collective-permute-start(f32[32,7,1280]{2,0,1:T(8,128)S(1)} %copy.26), channel_id=1, source_target_pairs={{1,0},{2,1},{3,2},{5,4},{6,5},{7,6},{9,8},{10,9},{11,10},{13,12},{... | collective-permute-start | bytes 3440648 | tf_op jit(solution)/shard_map/ppermute | solution.py:20
  266.5 18.4 %collective-permute-start.10 = (f32[15,16,1280]{2,1,0:T(8,128)S(1)}, f32[15,16,1280]{2,1,0:T(8,128)S(1)}, u32[]{:S(2)}, u32[]{:S(2)}) collective-permute-start(f32[15,16,1280]{2,1,0:T(8,128)S(1)} %get-tuple-element.10), channel_id=1, source_target_pairs={{0,4},{4,8},{8,12},{12,16},{16,20},{20,24},{24,28},{28,32},{32,36}... | collective-permute-start | bytes 3686408 | tf_op jit(solution)/shard_map/ppermute | solution.py:18
  271.1 18.1 %collective-permute-start.11 = (f32[15,16,1280]{2,1,0:T(8,128)S(1)}, f32[15,16,1280]{2,1,0:T(8,128)}, u32[]{:S(2)}, u32[]{:S(2)}) collective-permute-start(f32[15,16,1280]{2,1,0:T(8,128)S(1)} %get-tuple-element.11), channel_id=1, source_target_pairs={{4,0},{8,4},{12,8},{16,12},{20,16},{24,20},{28,24},{32,28},{36,32}... | collective-permute-start | bytes 3686408 | tf_op jit(solution)/shard_map/ppermute | solution.py:20
  345.8 18.7 %collective-permute-start.12 = (f32[15,16,1280]{2,1,0:T(8,128)S(1)}, f32[15,16,1280]{2,1,0:T(8,128)S(1)}, u32[]{:S(2)}, u32[]{:S(2)}) collective-permute-start(f32[15,16,1280]{2,1,0:T(8,128)S(1)} %get-tuple-element.8), channel_id=1, source_target_pairs={{0,4},{4,8},{8,12},{12,16},{16,20},{20,24},{24,28},{28,32},{32,36}... | collective-permute-start | bytes 3686408 | tf_op jit(solution)/shard_map/ppermute | solution.py:18
  349.5 19.4 %collective-permute-start.13 = (f32[15,16,1280]{2,1,0:T(8,128)S(1)}, f32[15,16,1280]{2,1,0:T(8,128)}, u32[]{:S(2)}, u32[]{:S(2)}) collective-permute-start(f32[15,16,1280]{2,1,0:T(8,128)S(1)} %get-tuple-element.9), channel_id=1, source_target_pairs={{4,0},{8,4},{12,8},{16,12},{20,16},{24,20},{28,24},{32,28},{36,32}... | collective-permute-start | bytes 3686408 | tf_op jit(solution)/shard_map/ppermute | solution.py:20
  421.7 15.1 %collective-permute-start.14 = (f32[32,7,1280]{2,0,1:T(8,128)S(1)}, f32[32,7,1280]{2,0,1:T(8,128)S(1)}, u32[]{:S(2)}, u32[]{:S(2)}) collective-permute-start(f32[32,7,1280]{2,0,1:T(8,128)S(1)} %copy.28), channel_id=1, source_target_pairs={{0,1},{1,2},{2,3},{4,5},{5,6},{6,7},{8,9},{9,10},{10,11},{12,13},{... | collective-permute-start | bytes 3440648 | tf_op jit(solution)/shard_map/ppermute | solution.py:18
  424.4 18.7 %collective-permute-start.15 = (f32[32,7,1280]{2,0,1:T(8,128)S(1)}, f32[32,7,1280]{2,0,1:T(8,128)S(1)}, u32[]{:S(2)}, u32[]{:S(2)}) collective-permute-start(f32[32,7,1280]{2,0,1:T(8,128)S(1)} %copy.30), channel_id=1, source_target_pairs={{1,0},{2,1},{3,2},{5,4},{6,5},{7,6},{9,8},{10,9},{11,10},{13,12},{... | collective-permute-start | bytes 3440648 | tf_op jit(solution)/shard_map/ppermute | solution.py:20
  535.5 2.1 copy-start.1
  535.5 213.0 %copy-start.7 = (s32[256]{0:T(256)S(1)}, s32[256]{0:T(256)}, u32[]{:S(2)}) copy-start(s32[256]{0:T(256)} %param.9) | copy-start | bytes 3076
  535.5 213.0 %copy-start.8 = (s32[8]{0:T(128)S(1)}, s32[8]{0:T(128)}, u32[]{:S(2)}) copy-start(s32[8]{0:T(128)} %param.8) | copy-start | bytes 100
  537.0 211.5 %reduce-scatter.5.cloned.1.call-start = ((), (), s32[]{:S(2)}) async-start(), calls=%async_computation.3 | async-start | bytes 40960 | tf_op jit(solution)/shard_map/reduce_scatter | solution.py:69
Sparse Core Ops, SparseCore 0:
  537.2 161.8 reduce-scatter.2
  701.6 46.9 reduce-scatter.4
